TPU v7x, 128 devices: a whole 4x4x4 slice. The times are simulated.
128 devices in a mesh: req: 8 (over y, core), hid: 16 (over x, z).
Axes of the slice: x: 4, y: 4, z: 4, core: 2. Of those that a mesh axis runs over, the one named last changes fastest.
Arguments:
- merged: bfloat16 [8, 256, 12800], P(None, 'req', 'hid')
- ln_gain: bfloat16 [12800], replicated, may hold values from 0.25 to 1.75
- ln_bias: bfloat16 [12800], replicated, may hold values from -3 to 3
- proj_weight: bfloat16 [12800, 6144], P(None, 'hid'), may hold values from -0.0546875 to 0.0546875
- proj_bias: float32 [6144], P('hid'), may hold values from -3 to 3
- text_embed: bfloat16 [16, 480, 6144], P('req', None, 'hid')
- attn_gain: bfloat16 [6144], replicated, may hold values from 0.25 to 1.75
- query_weight: bfloat16 [6144, 6144], P(None, 'hid')
- key_weight: bfloat16 [6144, 1024], P(None, 'hid')
- value_weight: bfloat16 [6144, 1024], P(None, 'hid'), may hold values from -0.078125 to 0.078125
- out_weight: bfloat16 [6144, 6144], P('hid'), may hold values from -0.078125 to 0.078125
- final_gain: bfloat16 [6144], replicated, may hold values from 0.25 to 1.75
- head_weight: bfloat16 [49152, 6144], P(('req', 'hid')), may hold values from -0.23925781 to 0.23925781
- lengths: int32 [16], P('req'), may hold values from 160 to 480, as said below
- tile_request: int32 [8], replicated, may hold values from 0 to 15, as said below
- insert_pos: int32 [8], replicated, may hold values from 0 to 224, as said below
Outputs:
- hidden: bfloat16 [16, 480, 6144], P('req', None, 'hid')
- final_norm: float32 [16], replicated
- logit_max: float32 [16], replicated
Inputs may be any that keep to these rules, and one draw needn't show every extreme that they name: For every g, the requests 2g and 2g + 1 have lengths that add up to exactly 640. `tile_request`: each pair of requests 2g, 2g + 1 holds exactly one tile, in the one of the two whose length is not smaller. insert_pos[t] + 256 is at most the length of request tile_request[t].
All inputs are finite; a program needn't handle non-finite values.
Results may differ from a plain program's by a relative error of at most 0.0095.
Values may be sent and summed in bfloat16 or wider, within the bound.
No kernel may reach another device: no remote copies, remote signals or barrier semaphores. Data moves between devices by JAX's collectives and lax.ppermute only.
A program may use at most 128 MiB of HBM per device.

v0:
```python
import math

import jax
import jax.numpy as jnp
from jax import lax
from jax.sharding import PartitionSpec as P

HEAD_DIM = 128
D = 6144
REQ_GRP = 2


def from_partner(block, axis, stride):
    count = lax.axis_size(axis)
    route = []
    for low in range(count):
        high = low | 1 << stride
        if high != low and high < count:
            route += [(low, high), (high, low)]
    return lax.ppermute(block, axis, route)


def rotary(values, positions):
    half_dim = values.shape[-1] // 2
    inv_freq = jnp.exp(
        jnp.arange(half_dim, dtype=jnp.float32) * (-2.0 * math.log(1000000.0) / values.shape[-1])
    )
    angles = positions.astype(jnp.float32)[:, None] * inv_freq[None, :]
    cosine = jnp.cos(angles)[:, None, :]
    sine_val = jnp.sin(angles)[:, None, :]
    first_half = values[..., :half_dim]
    second = values[..., half_dim:]
    return jnp.concatenate(
        [first_half * cosine - second * sine_val, second * cosine + first_half * sine_val], axis=-1
    )


def attend_local(queries, key_rows, value_rows, length):
    scores = jnp.einsum(
        "qhd,sd->hqs", queries, key_rows, preferred_element_type=jnp.float32
    ) / math.sqrt(HEAD_DIM)
    positions = jnp.arange(queries.shape[0])
    allowed = positions[None, :] <= positions[:, None]
    scores = jnp.where(allowed[None], scores, -jnp.inf)
    row_top = jnp.max(scores, axis=-1, keepdims=True)
    weights = jnp.exp(scores - row_top)
    weights = (weights / jnp.sum(weights, axis=-1, keepdims=True)).astype(jnp.bfloat16)
    mixed_out = jnp.einsum("hqs,sd->qhd", weights, value_rows, preferred_element_type=jnp.float32)
    mixed_out = jnp.where((positions < length)[:, None, None], mixed_out, 0.0)
    return mixed_out.reshape(queries.shape[0], -1).astype(jnp.bfloat16)


def shards(
    merged,
    ln_gain,
    ln_bias,
    proj_weight,
    proj_bias,
    text_embed,
    attn_gain,
    query_weight,
    key_weight,
    value_weight,
    out_weight,
    final_gain,
    head_weight,
    lengths,
    tile_request,
    insert_pos,
):
    owners = tile_request // REQ_GRP
    tile_order = jnp.argsort(owners)
    outgoing = merged[tile_order]
    arrived = lax.all_to_all(outgoing, "req", split_axis=0, concat_axis=1, tiled=True)
    features = lax.all_gather(arrived[0], "hid", axis=1, tiled=True)
    values = features.astype(jnp.float32)
    row_mean = jnp.mean(values, axis=1, keepdims=True)
    row_var = jnp.mean(values * values, axis=1, keepdims=True) - row_mean * row_mean
    normed = (
        (values - row_mean) * lax.rsqrt(row_var + 1e-05) * ln_gain.astype(jnp.float32)
        + ln_bias.astype(jnp.float32)
    ).astype(jnp.bfloat16)
    projected = jnp.dot(normed, proj_weight, preferred_element_type=jnp.float32) + proj_bias
    projected = jax.nn.gelu(projected, approximate=False).astype(jnp.bfloat16)
    own_tile = tile_order[lax.axis_index("req")]
    local_req = tile_request[own_tile] % REQ_GRP
    embedded = lax.dynamic_update_slice(
        text_embed, projected[None], (local_req, insert_pos[own_tile], jnp.zeros((), jnp.int32))
    )
    length_max = text_embed.shape[1]
    flat_rows = embedded.reshape(REQ_GRP * length_max, -1)
    position = jnp.arange(length_max)
    gain_part = attn_gain.astype(jnp.float32)
    portion_f = lax.all_gather(flat_rows, "hid", axis=1, tiled=True).astype(jnp.float32)
    scaled = (portion_f * gain_part).astype(jnp.bfloat16)
    squares = jnp.sum(portion_f * portion_f, axis=1)
    q_total = jnp.dot(scaled, query_weight, preferred_element_type=jnp.float32)
    k_total = jnp.dot(scaled, key_weight, preferred_element_type=jnp.float32)
    v_total = jnp.dot(scaled, value_weight, preferred_element_type=jnp.float32)
    row_scale = lax.rsqrt(squares / D + 1e-05)[:, None]
    queries = q_total * row_scale
    key_half = (k_total * row_scale).astype(jnp.bfloat16)
    value_half = (v_total * row_scale).astype(jnp.bfloat16)
    other_key, other_value = from_partner((key_half, value_half), "hid", 0)
    is_lower = lax.axis_index("hid") % 2 == 0
    key_raw = jnp.where(
        is_lower,
        jnp.concatenate([key_half, other_key], 1),
        jnp.concatenate([other_key, key_half], 1),
    )
    kv_values = jnp.where(
        is_lower,
        jnp.concatenate([value_half, other_value], 1),
        jnp.concatenate([other_value, value_half], 1),
    )
    heads_local = queries.shape[1] // HEAD_DIM
    queries = queries.reshape(REQ_GRP, length_max, heads_local, HEAD_DIM)
    key_raw = key_raw.reshape(REQ_GRP, length_max, 1, HEAD_DIM)
    kv_values = kv_values.reshape(REQ_GRP, length_max, HEAD_DIM)
    pieces = []
    for request in range(REQ_GRP):
        q_rotated = rotary(queries[request], position).astype(jnp.bfloat16)
        k_rotated = rotary(key_raw[request].astype(jnp.float32), position).astype(jnp.bfloat16)[
            :, 0, :
        ]
        pieces.append(attend_local(q_rotated, k_rotated, kv_values[request], lengths[request]))
    attended = jnp.concatenate(pieces, axis=0)
    partial_value = jnp.dot(attended, out_weight, preferred_element_type=jnp.float32)
    attn_sum = lax.psum_scatter(
        partial_value.astype(jnp.bfloat16), "hid", scatter_dimension=1, tiled=True
    ).astype(jnp.float32)
    hidden = (
        (flat_rows.astype(jnp.float32) + attn_sum)
        .astype(jnp.bfloat16)
        .reshape(REQ_GRP, length_max, -1)
    )
    last_rows = hidden[jnp.arange(REQ_GRP), lengths - 1]
    full_width = lax.all_gather(last_rows, "hid", axis=1, tiled=True)
    all_last = lax.all_gather(full_width, "req", axis=0, tiled=True)
    last_values = all_last.astype(jnp.float32)
    last_squares = jnp.sum(last_values * last_values, axis=1)
    final_norm = jnp.sqrt(last_squares)
    final_scaled = (
        last_values * lax.rsqrt(last_squares / D + 1e-05)[:, None] * final_gain.astype(jnp.float32)
    ).astype(jnp.bfloat16)
    logits = lax.dot_general(
        final_scaled, head_weight, (((1,), (1,)), ((), ())), preferred_element_type=jnp.float32
    )
    logit_max = lax.pmax(jnp.max(logits, axis=1), ("req", "hid"))
    return (hidden, final_norm, logit_max)


def solution(mesh):
    return jax.shard_map(
        shards,
        mesh=mesh,
        in_specs=(
            P(None, "req", "hid"),
            P(),
            P(),
            P(None, "hid"),
            P("hid"),
            P("req", None, "hid"),
            P(),
            P(None, "hid"),
            P(None, "hid"),
            P(None, "hid"),
            P("hid", None),
            P(),
            P(("req", "hid"), None),
            P("req"),
            P(),
            P(),
        ),
        out_specs=(P("req", None, "hid"), P(), P()),
        check_vma=False,
    )
```

profile of v0, /device:TPU:1, one launch (start us, length us, event | category | flops | bytes accessed | tf_op | source)
XLA Modules:
  0.0 487.0 jit_solution(6029854030120784377)
XLA Ops:
  7.2 0.7 and_select_fusion
  8.0 1.0 sort.17
  8.9 1.6 gather_fusion
  10.6 14.5 %all_to_all.4 = bf16[8,32,800]{2,1,0:T(8,128)(2,1)S(1)} all-to-all(bf16[8,32,800]{2,1,0:T(8,128)(2,1)S(1)} %gather_fusion), channel_id=1, replica_groups=mesh['req'=8,'hid'=16] {'req'}, dimensions={0} | all-to-all | bytes 819200 | tf_op jit(solution)/shard_map/all_to_all | solution.py:74
  25.1 0.9 copy.58
  26.1 0.6 dynamic_slice.9
  28.7 1.2 dynamic_slice.10
  31.9 1.2 dynamic_slice.11
  34.4 0.8 convert_element_type.138
  35.8 53.5 %all-gather.4.cloned.1.call-done = bf16[256,12800]{0,1:T(8,128)(2,1)} async-done(((bf16[256,800]{0,1:T(8,128)(2,1)}), bf16[256,12800]{0,1:T(8,128)(2,1)}) %all-gather.4.cloned.1.call-update) | async-done | bytes 6553616 | tf_op jit(solution)/shard_map/all_gather | solution.py:75
  89.4 4.9 %convert_reduce_fusion = (f32[256]{0:T(256)S(1)}, f32[256]{0:T(256)S(1)}) fusion(bf16[256,12800]{0,1:T(8,128)(2,1)} %all-gather.4.cloned.1.call-done), kind=kLoop, calls=%fused_computation.10 | loop fusion | flops 13106688 | bytes 6555648 | tf_op jit(solution)/shard_map/reduce_sum | solution.py:77
  94.3 15.5 %fusion.70 = bf16[1,256,384]{2,1,0:T(8,128)(2,1)S(1)} fusion(bf16[12800,384]{1,0:T(8,128)(2,1)} %param.19, bf16[256,12800]{0,1:T(8,128)(2,1)S(1)} %copy-done.6, f32[12800]{0:T(1024)S(1)} %convert_element_type.139, f32[12800]{0:T(1024)S(1)} %convert_element_type.138, f32[256]{0:T(256)S(1)} %get-tuple-element.30, f32[256]{0:T(256)S(1)} %get-tuple-element.29, ...), kind=kOutput, calls=%fused_computation.84 | convolution fusion | flops 2542731264 | bytes 16686592 | tf_op jit(solution)/shard_map/dot_general | solution.py:83
  109.9 1.5 dynamic_update_slice.3
  111.4 0.9 copy-done.3
  112.4 0.6 fusion.121
  113.1 1.2 iota_compare_fusion.2
  114.3 1.2 iota_compare_fusion.1
  115.5 0.8 iota_compare_fusion
  116.3 1.7 multiply_cosine_fusion
  118.0 88.9 %all-gather.6.cloned.1.call-done = bf16[960,6144]{1,0:T(8,128)(2,1)} async-done(((bf16[960,384]{1,0:T(8,128)(2,1)}), bf16[960,6144]{1,0:T(8,128)(2,1)}) %all-gather.6.cloned.1.call-update) | async-done | bytes 11796496 | tf_op jit(solution)/shard_map/all_gather | solution.py:94
  206.9 6.8 %fusion.3 = f32[960]{0:T(1024)S(1)} fusion(bf16[960,6144]{1,0:T(8,128)(2,1)} %all-gather.6.cloned.1.call-done), kind=kLoop, calls=%fused_computation.7 | loop fusion | flops 17693760 | bytes 11800320 | tf_op jit(solution)/shard_map/reduce_sum | solution.py:96
  213.7 8.1 %fusion.52 = bf16[960,64]{0,1:T(8,128)(2,1)S(1)} fusion(bf16[6144,64]{0,1:T(8,128)(2,1)S(1)} %copy-done, bf16[960,6144]{1,0:T(8,128)(2,1)} %all-gather.6.cloned.1.call-done, f32[6144]{0:T(1024)S(1)} %convert_element_type.144, f32[960]{0:T(1024)S(1)} %add_rsqrt_fusion), kind=kOutput, calls=%fused_computation.53 | convolution fusion | flops 772792320 | bytes 12734208 | tf_op jit(solution)/shard_map/dot_general | solution.py:98
  221.8 1.1 collective-permute-start.1
  222.9 6.3 %fusion.23 = f32[960,384]{1,0:T(8,128)S(1)} fusion(bf16[6144,384]{1,0:T(8,128)(2,1)S(1)} %bitcast.98, bf16[960,6144]{1,0:T(8,128)(2,1)S(1)} %copy-done.2, f32[6144]{0:T(1024)S(1)} %convert_element_type.144, f32[960]{0:T(1024)S(1)} %add_rsqrt_fusion), kind=kOutput, calls=%fused_computation.33 | convolution fusion | flops 4547911680 | bytes 18018048 | tf_op jit(solution)/shard_map/dot_general | solution.py:97
  229.3 0.3 copy.59
  230.2 0.3 copy.66
  231.1 8.2 %fusion.46 = bf16[960,64]{0,1:T(8,128)(2,1)S(1)} fusion(bf16[6144,64]{0,1:T(8,128)(2,1)} %param.25, bf16[960,6144]{1,0:T(8,128)(2,1)} %all-gather.6.cloned.1.call-done, f32[6144]{0:T(1024)S(1)} %convert_element_type.144, f32[960]{0:T(1024)S(1)} %add_rsqrt_fusion), kind=kOutput, calls=%fused_computation.51 | convolution fusion | flops 772792320 | bytes 12734208 | tf_op jit(solution)/shard_map/dot_general | solution.py:99
  239.3 0.9 collective-permute-start
  240.2 1.1 subtract_convert_fusion.1
  241.3 1.0 maximum_select_fusion.1
  242.5 0.6 fusion.108
  243.1 0.6 fusion.73
  243.8 1.5 fusion.123
  245.4 0.8 fusion.41
  246.4 0.6 fusion.77
  247.1 1.5 fusion.122
  248.6 0.8 fusion.42
  249.7 12.0 %convolution_convert_fusion = bf16[960,6144]{1,0:T(8,128)(2,1)} fusion(bf16[384,6144]{1,0:T(8,128)(2,1)} %param.26, bf16[480,384]{0,1:T(8,128)(2,1)S(1)} %bitcast.92, bf16[480,384]{0,1:T(8,128)(2,1)S(1)} %bitcast.91), kind=kOutput, calls=%fused_computation.16 | convolution fusion | flops 4537221120 | bytes 17252352 | tf_op jit(solution)/shard_map/dot_general | solution.py:128
  261.7 16.4 %copy.83 = bf16[960,6144]{0,1:T(8,128)(2,1)} copy(bf16[960,6144]{1,0:T(8,128)(2,1)} %convolution_convert_fusion) | data formatting | bytes 23592960
  278.2 0.7 copy-done.15
  278.9 94.6 %reduce-scatter.4.cloned.1.call-done = bf16[384,960]{1,0:T(8,128)(2,1)} async-done(((bf16[6144,960]{1,0:T(8,128)(2,1)}), bf16[384,960]{1,0:T(8,128)(2,1)}) %reduce-scatter.4.cloned.1.call-update) | async-done | bytes 737296
  373.5 1.6 copy.84
  375.3 0.6 gather_fusion.1
  376.0 15.6 %all_gather.14 = bf16[2,6144]{1,0:T(2,128)(2,1)S(1)} all-gather(bf16[2,384]{1,0:T(2,128)(2,1)S(1)} %gather_fusion.1), channel_id=1, replica_groups=mesh['req'=8,'hid'=16] {'hid'}, dimensions={1}, use_global_device_ids=true | all-gather | bytes 26112 | tf_op jit(solution)/shard_map/all_gather | solution.py:138
  391.5 20.6 %all-gather = bf16[8,2,6144]{2,1,0:T(2,128)(2,1)S(1)} all-gather(bf16[1,2,6144]{2,1,0:T(2,128)(2,1)S(1)} %bitcast.96), channel_id=1, replica_groups=mesh['req'=8,'hid'=16] {'req'}, dimensions={0}, use_global_device_ids=true | all-gather | bytes 221184 | tf_op jit(solution)/shard_map/all_gather | solution.py:139
  412.3 0.5 add_rsqrt_fusion.2
  412.9 3.8 convolution_reduce_fusion
  416.6 63.8 %pmax.7 = f32[16]{0:T(128)} all-reduce(f32[16]{0:T(128)S(1)} %convolution_reduce_fusion), channel_id=1, replica_groups=mesh['req'=8,'hid'=16] {'req','hid'}, use_global_device_ids=true, to_apply=%region_11.12 | all-reduce | flops 16 | bytes 128 | tf_op jit(solution)/shard_map/pmax | solution.py:149
  (82 shorter events, 2.6 us)
Async XLA Ops:
  7.2 206.5 %copy-start = (bf16[6144,64]{0,1:T(8,128)(2,1)S(1)}, bf16[6144,64]{0,1:T(8,128)(2,1)}, u32[]{:S(2)}) copy-start(bf16[6144,64]{0,1:T(8,128)(2,1)} %param.24) | copy-start | bytes 2359300
  7.2 28.0 %copy-start.13 = (bf16[12800]{0:T(1024)(128)(2,1)S(1)}, bf16[12800]{0:T(1024)(128)(2,1)}, u32[]{:S(2)}) copy-start(bf16[12800]{0:T(1024)(128)(2,1)} %param.18) | copy-start | bytes 76804
  7.2 82.2 %all-gather.4.cloned.1.call-start = ((), (), s32[]{:S(2)}) async-start(), calls=%async_computation.2 | async-start | bytes 6963200 | tf_op jit(solution)/shard_map/all_gather | solution.py:75
  10.6 83.7 %copy-start.20 = (f32[384]{0:T(512)S(1)}, f32[384]{0:T(512)}, u32[]{:S(2)}) copy-start(f32[384]{0:T(512)} %param.20) | copy-start | bytes 4612
  26.1 180.8 %all-gather.6.cloned.1.call-start = ((), (), s32[]{:S(2)}) async-start(), calls=%async_computation.3 | async-start | bytes 12533760 | tf_op jit(solution)/shard_map/all_gather | solution.py:94
  89.4 4.9 %copy-start.6 = (bf16[256,12800]{0,1:T(8,128)(2,1)S(1)}, bf16[256,12800]{0,1:T(8,128)(2,1)}, u32[]{:S(2)}) copy-start(bf16[256,12800]{0,1:T(8,128)(2,1)} %all-gather.4.cloned.1.call-done) | copy-start | bytes 19660804
  94.3 15.6 %copy-start.5 = (bf16[2,480,384]{2,1,0:T(8,128)(2,1)S(1)}, bf16[2,480,384]{2,1,0:T(8,128)(2,1)}, u32[]{:S(2)}) copy-start(bf16[2,480,384]{2,1,0:T(8,128)(2,1)} %param.21) | copy-start | bytes 2211844
  94.3 18.0 %copy-start.14 = (bf16[6144]{0:T(1024)(128)(2,1)S(1)}, bf16[6144]{0:T(1024)(128)(2,1)}, u32[]{:S(2)}) copy-start(bf16[6144]{0:T(1024)(128)(2,1)} %param.22) | copy-start | bytes 36868
  94.3 18.1 %copy-start.16 = (s32[2]{0:T(128)S(1)}, s32[2]{0:T(128)}, u32[]{:S(2)}) copy-start(s32[2]{0:T(128)} %param.29) | copy-start | bytes 28
  111.4 0.9 copy-start.3
  112.3 261.2 %reduce-scatter.4.cloned.1.call-start = ((), (), s32[]{:S(2)}) async-start(), calls=%async_computation.4 | async-start | bytes 13369344
  112.4 101.3 %copy-start.18 = (f32[64]{0:T(128)}, f32[64]{0:T(128)S(1)}, u32[]{:S(2)}) copy-start(f32[64]{0:T(128)S(1)} %multiply_exponential_fusion) | copy-start | bytes 772
  206.9 16.1 %slice-start = ((s8[4718592]{0:T(1024)(128)(4,1)}), s8[524288]{0:T(1024)(128)(4,1)S(1)}, s32[]{:S(2)}) async-start(s8[4718592]{0:T(1024)(128)(4,1)} %bitcast.97), calls=%async_computation.5 | async-start | bytes 1048576
  213.7 9.3 %copy-start.2 = (bf16[960,6144]{1,0:T(8,128)(2,1)S(1)}, bf16[960,6144]{1,0:T(8,128)(2,1)}, u32[]{:S(2)}) copy-start(bf16[960,6144]{1,0:T(8,128)(2,1)} %all-gather.6.cloned.1.call-done) | copy-start | bytes 35389444
  213.7 9.3 %slice-start.1 = ((s8[4718592]{0:T(1024)(128)(4,1)}), s8[4194304]{0:T(1024)(128)(4,1)S(1)}, s32[]{:S(2)}) async-start(s8[4718592]{0:T(1024)(128)(4,1)} %bitcast.97), calls=%async_computation.6 | async-start | bytes 8388608
  221.8 19.5 %collective-permute-start.1 = (bf16[960,64]{0,1:T(8,128)(2,1)S(1)}, bf16[960,64]{0,1:T(8,128)(2,1)}, u32[]{:S(2)}, u32[]{:S(2)}) collective-permute-start(bf16[960,64]{0,1:T(8,128)(2,1)S(1)} %fusion.52), channel_id=1, source_target_pairs={{0,1},{1,0},{2,3},{3,2},{4,5},{5,4},{6,7},{7,6},{8,9},{9,8},{10,11... | collective-permute-start | bytes 368648 | tf_op jit(solution)/shard_map/ppermute | solution.py:20
  231.1 9.1 %copy-start.8 = (f32[480,64]{1,0:T(8,128)S(1)}, f32[480,64]{1,0:T(8,128)}, u32[]{:S(2)}) copy-start(f32[480,64]{1,0:T(8,128)} %get-tuple-element.27) | copy-start | bytes 368644
  231.1 9.1 %copy-start.9 = (f32[480,64]{1,0:T(8,128)S(1)}, f32[480,64]{1,0:T(8,128)}, u32[]{:S(2)}) copy-start(f32[480,64]{1,0:T(8,128)} %get-tuple-element.28) | copy-start | bytes 368644
  239.3 3.2 copy-start.19
  239.3 6.0 %collective-permute-start = (bf16[960,64]{0,1:T(8,128)(2,1)S(1)}, bf16[960,64]{0,1:T(8,128)(2,1)S(1)}, u32[]{:S(2)}, u32[]{:S(2)}) collective-permute-start(bf16[960,64]{0,1:T(8,128)(2,1)S(1)} %fusion.46), channel_id=1, source_target_pairs={{0,1},{1,0},{2,3},{3,2},{4,5},{5,4},{6,7},{7,6},{8,9},{9,8},{10,11... | collective-permute-start | bytes 368648 | tf_op jit(solution)/shard_map/ppermute | solution.py:20
  240.2 3.5 copy-start.11
  243.8 1.6 copy-start.22
  245.4 1.0 copy-start.7
  245.4 1.7 copy-start.12
  246.4 2.2 copy-start.21
  278.1 0.7 copy-start.15
  278.1 0.7 copy-start.17
  278.1 96.9 %copy-start.4 = (bf16[2,480,384]{2,1,0:T(8,128)(2,1)S(1)}, bf16[2,480,384]{2,1,0:T(8,128)(2,1)}, u32[]{:S(2)}) copy-start(bf16[2,480,384]{2,1,0:T(8,128)(2,1)} %copy-done.3) | copy-start | bytes 2211844
  373.5 106.9 %copy-start.1 = (bf16[6144,64]{0,1:T(8,128)(2,1)S(1)}, bf16[6144,64]{0,1:T(8,128)(2,1)}, u32[]{:S(2)}) copy-start(bf16[6144,64]{0,1:T(8,128)(2,1)} %param.24) | copy-start | bytes 2359300
  375.3 105.1 %copy-start.10 = (bf16[960,384]{1,0:T(8,128)(2,1)}, bf16[960,384]{1,0:T(8,128)(2,1)S(1)}, u32[]{:S(2)}) copy-start(bf16[960,384]{1,0:T(8,128)(2,1)S(1)} %add_convert_fusion) | copy-start | bytes 2211844
Sparse Core Ops, SparseCore 0:
  26.2 63.1 all-gather.3
  112.4 94.4 all-gather.5
  278.3 95.1 reduce-scatter.3
where the time goes:
time: 488 us; the launch traced here: 487 us
  waiting for transfers between devices  237 us (49%)
  blocking collectives  114 us (23%)
  matrix products  56.8 us (12%)
  local copies, waits for them, and re-layouts  30.3 us (6%)
  other arithmetic  26 us (5%)
  between operations  20.1 us (4%)
    unnamed x4, waiting for transfers between devices  94.7 us
    all_gather x1, waiting for transfers between devices, shards(): lax.all_gather(flat_rows, 'hid', axis=1, tiled=True).astype(jnp.float32)  88.9 us
    pmax x1, blocking collectives, shards(): logit_max = lax.pmax(jnp.max(logits, axis=1), ('req', 'hid'))  63.8 us
    all_gather x1, waiting for transfers between devices, shards(): features = lax.all_gather(arrived[0], 'hid', axis=1, tiled=True)  53.5 us
    unnamed x56, local copies, waits for them, and re-layouts  20.7 us
    all_gather x1, blocking collectives, shards(): all_last = lax.all_gather(full_width, 'req', axis=0, tiled=True)  20.6 us
    all_gather x1, blocking collectives, shards(): full_width = lax.all_gather(last_rows, 'hid', axis=1, tiled=True)  15.6 us
    dot_general x1, matrix products, shards(): jnp.dot(normed, proj_weight, preferred_element_type=jnp.float32) + proj_bias  15.5 us
  transfers between devices with their start and end apart: 5, of which 3 were waited for; matrix products, arithmetic and copies ran while one was open for 6% of the time, Pallas kernels for 0%

commit v1 on v0

v1 whole, which is shorter than its diff:
```python
import math

import jax
import jax.numpy as jnp
from jax import lax
from jax.experimental import pallas as pl
from jax.experimental.pallas import tpu as pltpu
from jax.sharding import PartitionSpec as P

HEAD_DIM = 128
D = 6144
MERGED = 12800
REQ_GRP = 2
LEN_MAX = 480
LIVE = 640
TILE = 256
TEXT = LIVE - TILE
N_HID = 16
N_REQ = 8
RING = 4
FEAT = D // N_HID
MFEAT = MERGED // N_HID
MPAD = 896
BF = jnp.bfloat16
F32 = jnp.float32
VM = pltpu.VMEM


def vmem():
    return pl.BlockSpec(memory_space=pltpu.VMEM)


def params(mib):
    return pltpu.CompilerParams(vmem_limit_bytes=mib << 20)


def shift(block, dx, dz):
    route = []
    for i in range(N_HID):
        x, z = divmod(i, RING)
        route.append((((x + dx) % RING) * RING + (z + dz) % RING, i))
    return lax.ppermute(block, "hid", route)


def ring_gather(shard):
    half = shard.shape[0] // 2
    found = []
    for first in (0, 1):
        own = lax.slice_in_dim(shard, first * half, (first + 1) * half, axis=0)

        def inner(b, d):
            return shift(b, 0, d) if first == 0 else shift(b, d, 0)

        def outer(b, d):
            return shift(b, d, 0) if first == 0 else shift(b, 0, d)

        line = [(own, 0), (inner(own, -1), -1), (inner(own, 1), 1), (inner(own, 2), 2)]
        group = jnp.concatenate([b for b, _ in line], axis=0)
        minus = outer(group, -1)
        plus = outer(group, 1)
        far_a = outer(lax.slice_in_dim(minus, 0, 2 * half, axis=0), -1)
        far_b = outer(lax.slice_in_dim(plus, 2 * half, 4 * half, axis=0), 1)
        offs = [d for _, d in line]
        table = {}
        for array, out, part in (
            (group, 0, offs),
            (minus, -1, offs),
            (plus, 1, offs),
            (far_a, 2, offs[:2]),
            (far_b, 2, offs[2:]),
        ):
            found.append(array)
            for j, d in enumerate(part):
                rel = (out % RING, d % RING) if first == 0 else (d % RING, out % RING)
                table[rel] = (len(found) - 1, j * half)
        if first == 0:
            table_a = table
        else:
            table_b = table
    order = [(dx, dz) for dx in range(RING) for dz in range(RING)]
    return found, [(table_a[r], table_b[r]) for r in order]


def pack_kernel(order_ref, x_ref, o_ref):
    for g in range(N_REQ):
        rows = x_ref[order_ref[g]]
        v = rows.astype(F32)
        stats = []
        for s in (jnp.sum(v, axis=1, keepdims=True), jnp.sum(v * v, axis=1, keepdims=True)):
            for _ in range(3):
                part = s.astype(BF)
                stats.append(part)
                s = s - part.astype(F32)
        lo, hi = g * 32, (g + 1) * 32
        lane = lax.broadcasted_iota(jnp.int32, (32, MPAD - 768), 1)
        tail = jnp.zeros((32, MPAD - 768), F32)
        for j, part in enumerate(stats):
            tail = jnp.where(lane == 32 + j, part.astype(F32), tail)
        o_ref[lo:hi, 0:768] = rows[:, 0:768]
        o_ref[lo:hi, 768:MPAD] = tail.astype(BF)
        o_ref[lo:hi, 768:800] = rows[:, 768:800]


def pack(merged, tile_order):
    return pl.pallas_call(
        pack_kernel,
        out_shape=jax.ShapeDtypeStruct((TILE, MPAD), BF),
        in_specs=[pl.BlockSpec(memory_space=pltpu.SMEM), vmem()],
        out_specs=vmem(),
        compiler_params=params(16),
        name="pack",
    )(tile_order, merged)


def project_kernel(x_ref, st_ref, w_ref, g_ref, b_ref, pb_ref, o_ref, mean, rstd, acc):
    k = pl.program_id(0)

    @pl.when(k == 0)
    def _():
        total = jnp.zeros((TILE, 128), F32)
        for s in range(N_HID):
            total = total + st_ref[s * TILE : (s + 1) * TILE, :].astype(F32)
        m = jnp.sum(total[:, 32:35], axis=1, keepdims=True) * (1.0 / MERGED)
        q = jnp.sum(total[:, 35:38], axis=1, keepdims=True) * (1.0 / MERGED)
        mean[...] = jnp.broadcast_to(m, (TILE, 128))
        rstd[...] = jnp.broadcast_to(lax.rsqrt(q - m * m + 1e-05), (TILE, 128))
        acc[...] = jnp.zeros_like(acc)

    v = x_ref[:, 0:MFEAT].astype(F32)
    normed = (v - mean[:, 0:1]) * rstd[:, 0:1] * g_ref[0] + b_ref[0]
    acc[...] += jnp.dot(normed.astype(BF), w_ref[...], preferred_element_type=F32)

    @pl.when(k == N_HID - 1)
    def _():
        y = acc[...] + pb_ref[...]
        y = 0.5 * y * (1.0 + lax.erf(y * math.sqrt(0.5)))
        o_ref[...] = y.astype(BF)


def project(gathered, weight, gain, bias, out_bias):
    return pl.pallas_call(
        project_kernel,
        out_shape=jax.ShapeDtypeStruct((TILE, FEAT), BF),
        grid=(N_HID,),
        in_specs=[
            pl.BlockSpec((TILE, MPAD), lambda k: (k, 0)),
            pl.BlockSpec((N_HID * TILE, 128), lambda k: (0, 6)),
            pl.BlockSpec((MFEAT, FEAT), lambda k: (k, 0)),
            pl.BlockSpec((1, 1, MFEAT), lambda k: (k, 0, 0)),
            pl.BlockSpec((1, 1, MFEAT), lambda k: (k, 0, 0)),
            pl.BlockSpec((1, FEAT), lambda k: (0, 0)),
        ],
        out_specs=pl.BlockSpec((TILE, FEAT), lambda k: (0, 0)),
        scratch_shapes=[VM((TILE, 128), F32), VM((TILE, 128), F32), VM((TILE, FEAT), F32)],
        compiler_params=params(24),
        cost_estimate=pl.CostEstimate(
            flops=2 * TILE * MERGED * FEAT, bytes_accessed=17 << 20, transcendentals=0
        ),
        name="project",
    )(gathered, gathered, weight, gain, bias, out_bias)


def turn(v, cos, sin):
    return v * cos + pltpu.roll(v, HEAD_DIM // 2, 1) * sin


def qkv(shard, weight, gain, cos, sin, sources, name):
    rows = shard.shape[0]
    half = rows // 2
    arrays, where = ring_gather(shard)

    def kernel(src_ref, *refs):
        ins = refs[: len(arrays)]
        w_ref, g_ref, cos_ref, sin_ref, q_ref, kv_ref, xs, sq, acc = refs[len(arrays) :]
        k = pl.program_id(0)

        @pl.when(k == 0)
        def _():
            acc[...] = jnp.zeros_like(acc)
            sq[...] = jnp.zeros_like(sq)

        for i, places in enumerate(where):

            @pl.when(k == i)
            def _(places=places):
                for part, (a, row) in enumerate(places):
                    xs[part * half : (part + 1) * half, :] = ins[a][row : row + half, :]

        v = xs[...].astype(F32)
        w = v * v
        sq[...] += w[:, 0:128] + w[:, 128:256] + w[:, 256:384]
        scaled = (v * g_ref[0]).astype(BF)
        acc[...] += jnp.dot(scaled, w_ref[...], preferred_element_type=F32)

        @pl.when(k == N_HID - 1)
        def _():
            scale = lax.rsqrt(jnp.sum(sq[...], axis=1, keepdims=True) * (1.0 / D) + 1e-05)
            for h in range(FEAT // HEAD_DIM):
                part = acc[:, h * HEAD_DIM : (h + 1) * HEAD_DIM] * scale
                q_ref[:, h * HEAD_DIM : (h + 1) * HEAD_DIM] = turn(
                    part, cos_ref[...], sin_ref[...]
                ).astype(BF)
            kv_ref[...] = (acc[:, FEAT:] * scale).astype(BF)

    whole = lambda k, s: (0, 0)
    return pl.pallas_call(
        kernel,
        out_shape=(
            jax.ShapeDtypeStruct((rows, FEAT), BF),
            jax.ShapeDtypeStruct((rows, HEAD_DIM), BF),
        ),
        grid_spec=pltpu.PrefetchScalarGridSpec(
            num_scalar_prefetch=1,
            grid=(N_HID,),
            in_specs=[vmem() for _ in arrays]
            + [
                pl.BlockSpec((FEAT, FEAT + HEAD_DIM), lambda k, s: (s[k], 0)),
                pl.BlockSpec((1, 1, FEAT), lambda k, s: (s[k], 0, 0)),
                pl.BlockSpec((rows, HEAD_DIM), whole),
                pl.BlockSpec((rows, HEAD_DIM), whole),
            ],
            out_specs=(
                pl.BlockSpec((rows, FEAT), whole),
                pl.BlockSpec((rows, HEAD_DIM), whole),
            ),
            scratch_shapes=[
                VM((rows, FEAT), BF),
                VM((rows, HEAD_DIM), F32),
                VM((rows, FEAT + HEAD_DIM), F32),
            ],
        ),
        compiler_params=params(24),
        cost_estimate=pl.CostEstimate(
            flops=2 * rows * D * (FEAT + HEAD_DIM), bytes_accessed=12 << 20, transcendentals=0
        ),
        name=name,
    )(sources, *arrays, weight, gain, cos, sin)


def attend_kernel(
    low_ref, qt, qi, ot, pt, oi, pi, cos_ref, sin_ref, row_ref, col_ref, o_ref, keys, vals
):
    upper = low_ref[0] == 0
    lane = lax.broadcasted_iota(jnp.int32, (LIVE, HEAD_DIM), 1)
    own = jnp.concatenate([ot[...], oi[...]], axis=0).astype(F32)
    other = jnp.concatenate([pt[...], pi[...]], axis=0).astype(F32)
    low = jnp.where(upper, other, own)
    high = jnp.where(upper, own, other)
    key = jnp.where(lane < 64, low, pltpu.roll(high, 64, 1))
    val = jnp.where(lane < 64, pltpu.roll(low, 64, 1), high)
    keys[...] = turn(key, cos_ref[...], sin_ref[...]).astype(BF)
    vals[...] = val.astype(BF)
    code = col_ref[...]
    for blk in range(LIVE // 128):
        rows = slice(blk * 128, (blk + 1) * 128)
        mine = row_ref[rows, :]
        start = jnp.where(mine >= 1024, 1024, 0)
        live = jnp.logical_and(code <= mine, code >= start)
        for h in range(FEAT // HEAD_DIM):
            cols = slice(h * HEAD_DIM, (h + 1) * HEAD_DIM)
            if blk < TEXT // 128:
                q = qt[rows, cols]
            else:
                q = qi[blk * 128 - TEXT : blk * 128 - TEXT + 128, cols]
            s = lax.dot_general(
                q, keys[...], (((1,), (1,)), ((), ())), preferred_element_type=F32
            ) * (1.0 / math.sqrt(HEAD_DIM))
            s = jnp.where(live, s, -jnp.inf)
            w = jnp.exp(s - jnp.max(s, axis=1, keepdims=True))
            total = jnp.sum(w, axis=1, keepdims=True)
            mixed = jnp.dot(w.astype(BF), vals[...], preferred_element_type=F32)
            o_ref[rows, cols] = (mixed / total).astype(BF)


def attend(low, qt, qi, ot, pt, oi, pi, cos, sin, code):
    return pl.pallas_call(
        attend_kernel,
        out_shape=jax.ShapeDtypeStruct((LIVE, FEAT), BF),
        in_specs=[pl.BlockSpec(memory_space=pltpu.SMEM)] + [vmem()] * 10,
        out_specs=vmem(),
        scratch_shapes=[VM((LIVE, HEAD_DIM), BF), VM((LIVE, HEAD_DIM), BF)],
        compiler_params=params(24),
        cost_estimate=pl.CostEstimate(flops=1 << 30, bytes_accessed=2 << 20, transcendentals=0),
        name="attend",
    )(low, qt, qi, ot, pt, oi, pi, cos, sin, code[:, None], code[None, :])


def spread_kernel(a_ref, w_ref, o_ref):
    o_ref[0] = jnp.dot(a_ref[...], w_ref[...], preferred_element_type=F32).astype(BF)


def spread(attended, weight):
    return pl.pallas_call(
        spread_kernel,
        out_shape=jax.ShapeDtypeStruct((N_HID, LIVE, FEAT), BF),
        grid=(N_HID,),
        in_specs=[
            pl.BlockSpec((LIVE, FEAT), lambda k: (0, 0)),
            pl.BlockSpec((FEAT, FEAT), lambda k: (0, k)),
        ],
        out_specs=pl.BlockSpec((1, LIVE, FEAT), lambda k: (k, 0, 0)),
        compiler_params=params(24),
        cost_estimate=pl.CostEstimate(
            flops=2 * LIVE * FEAT * D, bytes_accessed=13 << 20, transcendentals=0
        ),
        name="spread",
    )(attended, weight)


def finish_kernel(text_ref, tile_ref, sum_ref, slot_ref, o_ref):
    for r in range(REQ_GRP):
        row = slot_ref[r]
        pick = (lax.broadcasted_iota(jnp.int32, (LEN_MAX, LIVE), 1) == row).astype(BF)
        moved = jnp.dot(pick, sum_ref[...], preferred_element_type=F32)
        image = jnp.dot(pick[:, TEXT:], tile_ref[...], preferred_element_type=F32)
        base = jnp.where(row >= TEXT, image, text_ref[r].astype(F32))
        o_ref[r] = (base + moved).astype(BF)


def finish(text, tile, sums, slots):
    return pl.pallas_call(
        finish_kernel,
        out_shape=jax.ShapeDtypeStruct((REQ_GRP, LEN_MAX, FEAT), BF),
        in_specs=[vmem()] * 4,
        out_specs=vmem(),
        compiler_params=params(24),
        name="finish",
    )(text, tile, sums, slots)


def shards(
    merged,
    ln_gain,
    ln_bias,
    proj_weight,
    proj_bias,
    text_embed,
    attn_gain,
    query_weight,
    key_weight,
    value_weight,
    out_weight,
    final_gain,
    head_weight,
    lengths,
    tile_request,
    insert_pos,
):
    hid = lax.axis_index("hid")
    me = lax.axis_index("req")
    owners = tile_request // REQ_GRP
    tiles = jnp.arange(N_REQ, dtype=jnp.int32)
    tile_order = jnp.sum(
        jnp.where(owners[None, :] == tiles[:, None], tiles[None, :], 0), axis=1
    ).astype(jnp.int32)
    mine = owners == me
    local_req = jnp.sum(jnp.where(mine, tile_request % REQ_GRP, 0))
    start = jnp.sum(jnp.where(mine, insert_pos, 0))
    len_a = lengths[0]
    first = local_req * len_a + start

    n = jnp.arange(LIVE, dtype=jnp.int32)
    packed = jnp.where(n < TEXT, jnp.where(n < first, n, n + TILE), n - TEXT + first)
    second = packed >= len_a
    pos = packed - jnp.where(second, len_a, 0)
    code = pos + jnp.where(second, 1024, 0)
    flat = pos + jnp.where(second, LEN_MAX, 0)
    slot = jnp.arange(LEN_MAX, dtype=jnp.int32)
    at = jnp.stack([slot, slot + len_a])
    in_tile = jnp.logical_and(at >= first, at < first + TILE)
    row_of = jnp.where(in_tile, at - first + TEXT, jnp.where(at < first, at, at - TILE))
    row_of = jnp.where(slot[None, :] < lengths[:, None], row_of, -1)

    half_dim = HEAD_DIM // 2
    inv_freq = jnp.exp(
        jnp.arange(half_dim, dtype=F32) * (-2.0 * math.log(1000000.0) / HEAD_DIM)
    )
    angles = pos.astype(F32)[:, None] * inv_freq[None, :]
    cosine, sine = jnp.cos(angles), jnp.sin(angles)
    cos = jnp.concatenate([cosine, cosine], axis=1)
    sin = jnp.concatenate([-sine, sine], axis=1)

    gathered = lax.all_gather(pack(merged, tile_order), "hid", axis=0, tiled=True)

    pick = (flat[:TEXT, None] == jnp.arange(REQ_GRP * LEN_MAX)[None, :]).astype(BF)
    text_rows = jnp.dot(
        pick, text_embed.reshape(REQ_GRP * LEN_MAX, FEAT), preferred_element_type=F32
    ).astype(BF)
    x, z = hid // RING, hid % RING
    rel = jnp.arange(N_HID, dtype=jnp.int32)
    sources = ((x + rel // RING) % RING) * RING + (z + rel % RING) % RING
    weight = jnp.concatenate([query_weight, key_weight, value_weight], axis=1)
    gain = attn_gain.astype(F32).reshape(N_HID, 1, FEAT)
    partner = [(i, i ^ 1) for i in range(N_HID)]

    q_text, kv_text = qkv(text_rows, weight, gain, cos[:TEXT], sin[:TEXT], sources, "qkv_text")
    other_text = lax.ppermute(kv_text, "hid", partner)

    projected = project(
        gathered,
        proj_weight,
        ln_gain.astype(F32).reshape(N_HID, 1, MFEAT),
        ln_bias.astype(F32).reshape(N_HID, 1, MFEAT),
        proj_bias[None, :],
    )
    tile = lax.all_to_all(
        projected.reshape(N_REQ, TILE // N_REQ, FEAT), "req", split_axis=0, concat_axis=0, tiled=True
    ).reshape(TILE, FEAT)
    q_tile, kv_tile = qkv(tile, weight, gain, cos[TEXT:], sin[TEXT:], sources, "qkv_tile")
    other_tile = lax.ppermute(kv_tile, "hid", partner)

    low = (hid % 2 == 0).astype(jnp.int32)[None]
    attended = attend(
        low, q_text, q_tile, kv_text, other_text, kv_tile, other_tile, cos, sin, code
    )
    partial = spread(attended, out_weight)
    sums = lax.psum_scatter(
        partial.reshape(N_HID * LIVE, FEAT), "hid", scatter_dimension=0, tiled=True
    )
    hidden = finish(text_embed, tile, sums, row_of[:, :, None])

    last = jnp.sum(jnp.where(slot[None, :] == lengths[:, None] - 1, row_of, 0), axis=1)
    pick_last = (last[:, None] == n[None, :]).astype(BF)
    rows_last = jnp.dot(pick_last, attended, preferred_element_type=F32).astype(BF)
    term = jnp.dot(rows_last, out_weight, preferred_element_type=F32).astype(BF)
    term = term.reshape(REQ_GRP, N_HID, FEAT).transpose(1, 0, 2)
    terms = lax.all_to_all(term, "hid", split_axis=0, concat_axis=0, tiled=True)
    base = jnp.dot(pick_last[:, :TEXT], text_rows, preferred_element_type=F32) + jnp.dot(
        pick_last[:, TEXT:], tile, preferred_element_type=F32
    )
    last_own = (base + jnp.sum(terms.astype(F32), axis=0)).astype(BF)
    full_width = lax.all_gather(last_own, "hid", axis=1, tiled=True)
    all_last = lax.all_gather(full_width, "req", axis=0, tiled=True)
    last_values = all_last.astype(F32)
    last_squares = jnp.sum(last_values * last_values, axis=1)
    final_norm = jnp.sqrt(last_squares)
    final_scaled = (
        last_values * lax.rsqrt(last_squares / D + 1e-05)[:, None] * final_gain.astype(F32)
    ).astype(BF)
    logits = lax.dot_general(
        final_scaled, head_weight, (((1,), (1,)), ((), ())), preferred_element_type=F32
    )
    top = jnp.max(logits, axis=1)
    top = jnp.max(lax.all_gather(top, "hid", axis=0), axis=0)
    logit_max = jnp.max(lax.all_gather(top, "req", axis=0), axis=0)
    return (hidden, final_norm, logit_max)


def solution(mesh):
    return jax.shard_map(
        shards,
        mesh=mesh,
        in_specs=(
            P(None, "req", "hid"),
            P(),
            P(),
            P(None, "hid"),
            P("hid"),
            P("req", None, "hid"),
            P(),
            P(None, "hid"),
            P(None, "hid"),
            P(None, "hid"),
            P("hid", None),
            P(),
            P(("req", "hid"), None),
            P("req"),
            P(),
            P(),
        ),
        out_specs=(P("req", None, "hid"), P(), P()),
        check_vma=False,
    )
```

time: 488 us -> 351 us (0.72)
  waiting for transfers between devices: 237 us -> 69.7 us
  starting transfers between devices: 2.14 us -> 50.9 us
  matrix products: 56.8 us -> 9.67 us
  Pallas kernels: 0 us -> 46 us
  blocking collectives: 114 us -> 93.8 us
  local copies, waits for them, and re-layouts: 30.3 us -> 37.9 us
    all_gather x2 -> x1, waiting for transfers between devices: 142 us -> 42.8 us  [shards(): lax.all_gather(pack(merged, tile_order), 'hid', axis=0, tiled=True)]
    unnamed x4 -> x2, waiting for transfers between devices: 94.7 us -> 0.03 us
    pmax x1 -> x0, blocking collectives: 63.8 us -> none  [shards(): logit_max = lax.pmax(jnp.max(logits, axis=1), ('req', 'hid'))]
    unnamed x0 -> x2, blocking collectives: none -> 50.1 us
    dot_general x9 -> x4, matrix products: 53 us -> 5.88 us  [the longest x1 3.86 us: shards(): term = jnp.dot(rows_last, out_weight, preferred_element_type=F32).astype(BF)]
    pallas_call x0 -> x7, Pallas kernels: none -> 46 us  [the longest x2 20.2 us: qkv(): pl.pallas_call(kernel, out_shape=(jax.ShapeDtypeStruct((rows, FEAT), BF),...]
    ppermute x2 -> x30, starting transfers between devices: 2.02 us -> 42.3 us  [the longest x28 40.8 us: shift(): return lax.ppermute(block, 'hid', route)]
    ppermute x2 -> x30, waiting for transfers between devices: 0.01 us -> 23.2 us  [the longest x28 21.2 us: shift(): return lax.ppermute(block, 'hid', route)]
  transfers between devices with their start and end apart: 5 -> 34, of which waited for: 3 -> 6; matrix products, arithmetic and copies ran while one was open for 6% -> 14% of each run, Pallas kernels for 0% -> 8%
where the time goes in v1:
time: 351 us; the launch traced here: 350 us
  blocking collectives  93.8 us (27%)
  waiting for transfers between devices  69.7 us (20%)
  starting transfers between devices  50.9 us (15%)
  Pallas kernels  46 us (13%)
  local copies, waits for them, and re-layouts  37.9 us (11%)
  other arithmetic  23.9 us (7%)
  between operations  17.9 us (5%)
  matrix products  9.67 us (3%)
    unnamed x2, blocking collectives  50.1 us
    all_gather x1, waiting for transfers between devices, shards(): lax.all_gather(pack(merged, tile_order), 'hid', axis=0, tiled=True)  42.8 us
    ppermute x28, starting transfers between devices, shift(): return lax.ppermute(block, 'hid', route)  40.8 us
    all_gather x1, blocking collectives, shards(): all_last = lax.all_gather(full_width, 'req', axis=0, tiled=True)  26.1 us
    unnamed x74, local copies, waits for them, and re-layouts  25.4 us
    ppermute x28, waiting for transfers between devices, shift(): return lax.ppermute(block, 'hid', route)  21.2 us
    pallas_call x2, Pallas kernels, qkv(): pl.pallas_call(kernel, out_shape=(jax.ShapeDtypeStruct((rows, FEAT), BF),...  20.2 us
    all_gather x1, blocking collectives, shards(): full_width = lax.all_gather(last_own, 'hid', axis=1, tiled=True)  17.6 us
  transfers between devices with their start and end apart: 34, of which 6 were waited for; matrix products, arithmetic and copies ran while one was open for 14% of the time, Pallas kernels for 8%

profile of v1, /device:TPU:1, one launch (start us, length us, event | category | flops | bytes accessed | tf_op | source)
XLA Modules:
  0.0 349.8 jit_solution(1874678593334871753)
XLA Ops:
  9.7 1.5 pack.1
  13.8 1.7 fusion.1
  16.3 2.0 collective-permute-start.7
  19.7 1.7 collective-permute-start.9
  21.4 1.6 collective-permute-start
  23.0 2.1 collective-permute-start.1
  27.6 1.9 copy.40
  29.5 1.9 copy.41
  31.5 7.4 %pad_maximum_fusion.refs_10_ = bf16[6144,512]{1,0:T(8,128)(2,1)} fusion(bf16[6144,64]{1,0:T(8,128)(2,1)S(1)} %copy.41, bf16[6144,64]{1,0:T(8,128)(2,1)S(1)} %copy.40, bf16[6144,384]{1,0:T(8,128)(2,1)} %param.23), kind=kLoop, calls=%fused_computation.1 | loop fusion | flops 18874368 | bytes 12582912 | tf_op jit(solution)/shard_map/concatenate | solution.py:392
  38.9 42.8 %all-gather.5.cloned.1.call-done.x_ref.st_ref = bf16[4096,896]{1,0:T(8,128)(2,1)} async-done(((bf16[256,896]{1,0:T(8,128)(2,1)}), bf16[4096,896]{1,0:T(8,128)(2,1)}) %all-gather.5.cloned.1.call-update) | async-done | bytes 7340048 | tf_op jit(solution)/shard_map/all_gather | solution.py:383
  81.7 3.1 copy-done.2
  84.8 3.8 %copy-done.3 = bf16[12800,384]{1,0:T(8,128)(2,1)S(1)} copy-done((bf16[12800,384]{1,0:T(8,128)(2,1)S(1)}, bf16[12800,384]{1,0:T(8,128)(2,1)}, u32[]{:S(2)}) %copy-start.3) | copy-done | bytes 9830424
  88.6 9.3 %project.1 = bf16[256,384]{1,0:T(8,128)(2,1)} custom-call(bf16[4096,896]{1,0:T(8,128)(2,1)S(1)} %copy-done.2, bf16[4096,896]{1,0:T(8,128)(2,1)S(1)} %copy-done.2, bf16[12800,384]{1,0:T(8,128)(2,1)S(1)} %copy-done.3, f32[16,1,800]{2,1,0:T(1,128)S(1)} %reshape.318.g_ref, f32[16,1,800]{2,1,0:T(1,128)S(1)} %reshape.320.b_ref, f32[1,384]{1,0:T(1,128)S(1)} %broadcast_in_dim.74.pb_ref), custom_call_target="tpu_custom_call" | custom-call | flops 2516582400 | bytes 17825792 | tf_op jit(solution)/shard_map/project/pallas_call | solution.py:141
  97.9 5.0 %all-to-all-start = ((bf16[8,32,384]{2,1,0:T(8,128)(2,1)}), bf16[8,32,384]{2,1,0:T(8,128)(2,1)S(1)}, u32[]{:S(2)}, u32[]{:S(2)}) async-start(bf16[8,32,384]{2,1,0:T(8,128)(2,1)} %bitcast), calls=%async_computation | async-start | bytes 393216 | tf_op jit(solution)/shard_map/all_to_all | solution.py:406
  104.1 2.7 collective-permute-start.2
  108.5 2.3 collective-permute-start.11
  111.7 2.7 collective-permute-start.15
  114.4 11.8 %collective-permute-done.14 = bf16[128,384]{1,0:T(8,128)(2,1)S(1)} collective-permute-done((bf16[128,384]{1,0:T(8,128)(2,1)S(1)}, bf16[128,384]{1,0:T(8,128)(2,1)S(1)}, u32[]{:S(2)}, u32[]{:S(2)}) %collective-permute-start.14) | collective-permute-done | bytes 98336 | tf_op jit(solution)/shard_map/ppermute | solution.py:42
  128.6 1.5 collective-permute-start.3
  131.4 1.4 collective-permute-start.23
  133.9 2.2 collective-permute-start.4
  136.1 9.0 %collective-permute-done.23 = bf16[128,384]{1,0:T(8,128)(2,1)S(1)} collective-permute-done((bf16[128,384]{1,0:T(8,128)(2,1)S(1)}, bf16[128,384]{1,0:T(8,128)(2,1)S(1)}, u32[]{:S(2)}, u32[]{:S(2)}) %collective-permute-start.23) | collective-permute-done | bytes 98336 | tf_op jit(solution)/shard_map/ppermute | solution.py:42
  145.9 2.7 collective-permute-start.18
  149.2 1.7 fusion.11.refs_13_
  151.7 2.0 pad_maximum_fusion.6.sin_ref
  153.7 2.1 collective-permute-start.25
  158.0 1.9 slice.89
  160.6 1.7 slice.90
  162.3 2.0 collective-permute-start.13
  164.7 2.3 collective-permute-start.6
  172.3 2.7 collective-permute-start.20
  175.0 2.7 collective-permute-start.27
  177.7 2.8 copy-done
  185.5 10.6 %qkv_text.1 = (bf16[384,384]{1,0:T(8,128)(2,1)S(1)}, bf16[384,128]{1,0:T(8,128)(2,1)S(1)}) custom-call(s32[16]{0:T(128)S(1)} %fusion.23.src_ref, bf16[768,384]{1,0:T(8,128)(2,1)S(1)} %pad_maximum_fusion.1.refs_0_, bf16[768,384]{1,0:T(8,128)(2,1)S(1)} %copy-done.9, bf16[768,384]{1,0:T(8,128)(2,1)} %collective-permute-done.4.refs_2_, ...), custom_call_target="tpu_custom_call" | custom-call | flops 2415919104 | bytes 12582912 | tf_op jit(solution)/shard_map/qkv_text/pallas_call | solution.py:206
  196.4 9.6 %qkv_tile.1 = (bf16[256,384]{1,0:T(8,128)(2,1)S(1)}, bf16[256,128]{1,0:T(8,128)(2,1)S(1)}) custom-call(s32[16]{0:T(128)S(1)} %fusion.23.src_ref, bf16[512,384]{1,0:T(8,128)(2,1)} %pad_maximum_fusion.3.refs_0_, bf16[512,384]{1,0:T(8,128)(2,1)} %collective-permute-done.17.refs_1_, bf16[512,384]{1,0:T(8,128)(2,1)} %collective-permute-done.18.refs_2_, ...), custom_call_target="tpu_custom_call" | custom-call | flops 1610612736 | bytes 12582912 | tf_op jit(solution)/shard_map/qkv_tile/pallas_call | solution.py:206
  207.4 2.0 collective-permute-done.29.pi
  209.4 5.1 %attend.1.a_ref = bf16[640,384]{1,0:T(8,128)(2,1)S(1)} custom-call(s32[1]{0:T(128)} %bitcast.2.low_ref, bf16[384,384]{1,0:T(8,128)(2,1)S(1)} %get-tuple-element.7.qt, bf16[256,384]{1,0:T(8,128)(2,1)S(1)} %get-tuple-element.8.qi, bf16[384,128]{1,0:T(8,128)(2,1)S(1)} %get-tuple-element.9.ot, bf16[384,128]{1,0:T(8,128)(2,1)S(1)} %collective-permute-done.28.pt, ...), custom_call_target="tpu_custom_call" | custom-call | flops 1073741824 | bytes 2097152 | tf_op jit(solution)/shard_map/attend/pallas_call | solution.py:276
  214.5 7.8 %spread.1 = bf16[16,640,384]{2,1,0:T(8,128)(2,1)S(1)} custom-call(bf16[640,384]{1,0:T(8,128)(2,1)S(1)} %attend.1.a_ref, bf16[384,6144]{1,0:T(8,128)(2,1)S(1)} %bitcast.28), custom_call_target="tpu_custom_call" | custom-call | flops 3019898880 | bytes 13631488 | tf_op jit(solution)/shard_map/spread/pallas_call | solution.py:293
  222.4 3.1 copy-done.1
  226.3 3.9 %convolution_convert_fusion = bf16[2,6144]{1,0:T(2,128)(2,1)} fusion(bf16[384,6144]{1,0:T(8,128)(2,1)} %w_ref.3, bf16[640,384]{1,0:T(8,128)(2,1)S(1)} %attend.1.a_ref, s32[2]{0:T(128)S(1)} %fusion.16), kind=kOutput, calls=%fused_computation | convolution fusion | flops 10434560 | bytes 5234696 | tf_op jit(solution)/shard_map/dot_general | solution.py:425
  230.1 3.6 %all-to-all-start.1 = ((bf16[16,2,384]{2,1,0:T(2,128)(2,1)}), bf16[16,2,384]{2,1,0:T(2,128)(2,1)S(1)}, u32[]{:S(2)}, u32[]{:S(2)}) async-start(bf16[16,2,384]{2,1,0:T(2,128)(2,1)} %bitcast.11), calls=%async_computation.2 | async-start | bytes 49152 | tf_op jit(solution)/shard_map/all_to_all | solution.py:427
  236.4 3.7 %all-to-all-done.1 = bf16[16,2,384]{2,1,0:T(2,128)(2,1)S(1)} async-done(((bf16[16,2,384]{2,1,0:T(2,128)(2,1)}), bf16[16,2,384]{2,1,0:T(2,128)(2,1)S(1)}, u32[]{:S(2)}, u32[]{:S(2)}) %all-to-all-start.1) | async-done | bytes 24608 | tf_op jit(solution)/shard_map/all_to_all | solution.py:427
  240.3 17.6 %all_gather.22 = bf16[2,6144]{1,0:T(2,128)(2,1)S(1)} all-gather(bf16[2,384]{1,0:T(2,128)(2,1)S(1)} %fusion.3), channel_id=1, replica_groups=mesh['req'=8,'hid'=16] {'hid'}, dimensions={1}, use_global_device_ids=true | all-gather | bytes 26112 | tf_op jit(solution)/shard_map/all_gather | solution.py:432
  257.9 26.1 %all-gather.2 = bf16[8,2,6144]{2,1,0:T(2,128)(2,1)S(1)} all-gather(bf16[1,2,6144]{2,1,0:T(2,128)(2,1)S(1)} %bitcast.42), channel_id=1, replica_groups=mesh['req'=8,'hid'=16] {'req'}, dimensions={0}, use_global_device_ids=true | all-gather | bytes 221184 | tf_op jit(solution)/shard_map/all_gather | solution.py:433
  284.8 3.8 %convolution_reduce_fusion = f32[16]{0:T(128)S(1)} fusion(bf16[384,6144]{1,0:T(8,128)(2,1)} %param.28, f32[16,6144]{1,0:T(8,128)S(1)} %reshape.334, f32[6144]{0:T(1024)S(1)} %convert_element_type.44, f32[16]{0:T(128)S(1)} %get-tuple-element.21), kind=kOutput, calls=%fused_computation.6 | convolution fusion | flops 75798512 | bytes 5136512 | tf_op jit(solution)/shard_map/dot_general | solution.py:440
  288.8 31.3 %all-reduce = f32[256]{0:T(256)S(1)} all-reduce(f32[256]{0:T(256)S(1)} %dynamic-update-slice), channel_id=2, replica_groups=mesh['req'=8,'hid'=16] {'hid'}, use_global_device_ids=true, to_apply=%add | all-reduce | flops 256 | bytes 2048
  320.4 18.8 %all-reduce.1 = f32[128]{0:T(128)S(1)} all-reduce(f32[128]{0:T(128)S(1)} %dynamic-update-slice.1), channel_id=3, replica_groups=mesh['req'=8,'hid'=16] {'req'}, use_global_device_ids=true, to_apply=%add.1 | all-reduce | flops 128 | bytes 1024
  340.9 2.1 finish.1
  (166 shorter events, 39.0 us)
Async XLA Ops:
  7.2 74.5 %all-gather.5.cloned.1.call-start = ((), (), s32[]{:S(2)}) async-start(), calls=%async_computation.3 | async-start | bytes 7798784 | tf_op jit(solution)/shard_map/all_gather | solution.py:383
  16.3 87.8 %copy-start.23 = (bf16[192,384]{1,0:T(8,128)(2,1)}, bf16[192,384]{1,0:T(8,128)(2,1)S(1)}, u32[]{:S(2)}) copy-start(bf16[192,384]{1,0:T(8,128)(2,1)S(1)} %get-tuple-element.15) | copy-start | bytes 442372
  16.3 87.8 %collective-permute-start.7 = (bf16[192,384]{1,0:T(8,128)(2,1)}, bf16[192,384]{1,0:T(8,128)(2,1)}, u32[]{:S(2)}, u32[]{:S(2)}) collective-permute-start(bf16[192,384]{1,0:T(8,128)(2,1)} %get-tuple-element.14), channel_id=1, source_target_pairs={{12,0},{13,1},{14,2},{15,3},{0,4},{1,5},{2,6},{3,7},{4,8},{5,9},{6... | collective-permute-start | bytes 442376 | tf_op jit(solution)/shard_map/ppermute | solution.py:42
  18.4 88.4 %collective-permute-start.8 = (bf16[192,384]{1,0:T(8,128)(2,1)}, bf16[192,384]{1,0:T(8,128)(2,1)}, u32[]{:S(2)}, u32[]{:S(2)}) collective-permute-start(bf16[192,384]{1,0:T(8,128)(2,1)} %get-tuple-element.14), channel_id=1, source_target_pairs={{4,0},{5,1},{6,2},{7,3},{8,4},{9,5},{10,6},{11,7},{12,8},{13,9},{1... | collective-permute-start | bytes 442376 | tf_op jit(solution)/shard_map/ppermute | solution.py:42
  19.7 87.2 %collective-permute-start.9 = (bf16[192,384]{1,0:T(8,128)(2,1)}, bf16[192,384]{1,0:T(8,128)(2,1)}, u32[]{:S(2)}, u32[]{:S(2)}) collective-permute-start(bf16[192,384]{1,0:T(8,128)(2,1)} %get-tuple-element.14), channel_id=1, source_target_pairs={{8,0},{9,1},{10,2},{11,3},{12,4},{13,5},{14,6},{15,7},{0,8},{1,9},... | collective-permute-start | bytes 442376 | tf_op jit(solution)/shard_map/ppermute | solution.py:42
  21.4 89.4 %collective-permute-start = (bf16[192,384]{1,0:T(8,128)(2,1)S(1)}, bf16[192,384]{1,0:T(8,128)(2,1)}, u32[]{:S(2)}, u32[]{:S(2)}) collective-permute-start(bf16[192,384]{1,0:T(8,128)(2,1)S(1)} %get-tuple-element.15), channel_id=1, source_target_pairs={{3,0},{0,1},{1,2},{2,3},{7,4},{4,5},{5,6},{6,7},{11,8},{8,9},{9,10... | collective-permute-start | bytes 442376 | tf_op jit(solution)/shard_map/ppermute | solution.py:42
  23.0 88.7 %collective-permute-start.1 = (bf16[192,384]{1,0:T(8,128)(2,1)S(1)}, bf16[192,384]{1,0:T(8,128)(2,1)}, u32[]{:S(2)}, u32[]{:S(2)}) collective-permute-start(bf16[192,384]{1,0:T(8,128)(2,1)S(1)} %get-tuple-element.15), channel_id=1, source_target_pairs={{1,0},{2,1},{3,2},{0,3},{5,4},{6,5},{7,6},{4,7},{9,8},{10,9},{11,1... | collective-permute-start | bytes 442376 | tf_op jit(solution)/shard_map/ppermute | solution.py:42
  97.9 12.9 %all-to-all-start = ((bf16[8,32,384]{2,1,0:T(8,128)(2,1)}), bf16[8,32,384]{2,1,0:T(8,128)(2,1)S(1)}, u32[]{:S(2)}, u32[]{:S(2)}) async-start(bf16[8,32,384]{2,1,0:T(8,128)(2,1)} %bitcast), calls=%async_computation | async-start | bytes 393216 | tf_op jit(solution)/shard_map/all_to_all | solution.py:406
  102.9 237.0 %reduce-scatter.2.cloned.1.call-start = ((), (), s32[]{:S(2)}) async-start(), calls=%async_computation.4 | async-start | bytes 8355840 | tf_op jit(solution)/shard_map/reduce_scatter | solution.py:417
  104.1 22.1 %copy-start.20 = (f32[640,64]{1,0:T(8,128)}, f32[640,64]{1,0:T(8,128)S(1)}, u32[]{:S(2)}) copy-start(f32[640,64]{1,0:T(8,128)S(1)} %get-tuple-element.19) | copy-start | bytes 491524
  104.1 24.5 %copy-start.19 = (f32[640,64]{1,0:T(8,128)}, f32[640,64]{1,0:T(8,128)S(1)}, u32[]{:S(2)}) copy-start(f32[640,64]{1,0:T(8,128)S(1)} %get-tuple-element.18) | copy-start | bytes 491524
  104.1 53.2 %copy-start.18 = (f32[640,64]{1,0:T(8,128)}, f32[640,64]{1,0:T(8,128)S(1)}, u32[]{:S(2)}) copy-start(f32[640,64]{1,0:T(8,128)S(1)} %get-tuple-element.20) | copy-start | bytes 491524
  104.1 10.2 %collective-permute-start.2 = (bf16[192,384]{1,0:T(8,128)(2,1)S(1)}, bf16[192,384]{1,0:T(8,128)(2,1)S(1)}, u32[]{:S(2)}, u32[]{:S(2)}) collective-permute-start(bf16[192,384]{1,0:T(8,128)(2,1)S(1)} %get-tuple-element.15), channel_id=1, source_target_pairs={{2,0},{3,1},{0,2},{1,3},{6,4},{7,5},{4,6},{5,7},{10,8},{11,9},{8,1... | collective-permute-start | bytes 442376 | tf_op jit(solution)/shard_map/ppermute | solution.py:42
  108.0 59.0 %copy-start.25 = (bf16[6144]{0:T(1024)(128)(2,1)S(1)}, bf16[6144]{0:T(1024)(128)(2,1)}, u32[]{:S(2)}) copy-start(bf16[6144]{0:T(1024)(128)(2,1)} %param.22) | copy-start | bytes 36868
  108.0 37.9 %collective-permute-start.10 = (bf16[768,384]{1,0:T(8,128)(2,1)S(1)}, bf16[768,384]{1,0:T(8,128)(2,1)S(1)}, u32[]{:S(2)}, u32[]{:S(2)}) collective-permute-start(bf16[768,384]{1,0:T(8,128)(2,1)S(1)} %pad_maximum_fusion.2.refs_5_), channel_id=1, source_target_pairs={{3,0},{0,1},{1,2},{2,3},{7,4},{4,5},{5,6},{6,7},{11,8},{8,9},{9,10... | collective-permute-start | bytes 1769480 | tf_op jit(solution)/shard_map/ppermute | solution.py:42
  108.5 40.1 %collective-permute-start.11 = (bf16[768,384]{1,0:T(8,128)(2,1)S(1)}, bf16[768,384]{1,0:T(8,128)(2,1)S(1)}, u32[]{:S(2)}, u32[]{:S(2)}) collective-permute-start(bf16[768,384]{1,0:T(8,128)(2,1)S(1)} %pad_maximum_fusion.2.refs_5_), channel_id=1, source_target_pairs={{1,0},{2,1},{3,2},{0,3},{5,4},{6,5},{7,6},{4,7},{9,8},{10,9},{11,1... | collective-permute-start | bytes 1769480 | tf_op jit(solution)/shard_map/ppermute | solution.py:42
  110.8 15.3 %collective-permute-start.14 = (bf16[128,384]{1,0:T(8,128)(2,1)S(1)}, bf16[128,384]{1,0:T(8,128)(2,1)S(1)}, u32[]{:S(2)}, u32[]{:S(2)}) collective-permute-start(bf16[128,384]{1,0:T(8,128)(2,1)S(1)} %bitcast.38), channel_id=1, source_target_pairs={{3,0},{0,1},{1,2},{2,3},{7,4},{4,5},{5,6},{6,7},{11,8},{8,9},{9,10... | collective-permute-start | bytes 294920 | tf_op jit(solution)/shard_map/ppermute | solution.py:42
  110.9 57.3 %copy-start.24 = (s32[2]{0:T(128)S(1)}, s32[2]{0:T(128)}, u32[]{:S(2)}) copy-start(s32[2]{0:T(128)} %param.29) | copy-start | bytes 28
  111.7 16.9 %collective-permute-start.15 = (bf16[128,384]{1,0:T(8,128)(2,1)S(1)}, bf16[128,384]{1,0:T(8,128)(2,1)S(1)}, u32[]{:S(2)}, u32[]{:S(2)}) collective-permute-start(bf16[128,384]{1,0:T(8,128)(2,1)S(1)} %bitcast.39), channel_id=1, source_target_pairs={{1,0},{2,1},{3,2},{0,3},{5,4},{6,5},{7,6},{4,7},{9,8},{10,9},{11,1... | collective-permute-start | bytes 294920 | tf_op jit(solution)/shard_map/ppermute | solution.py:42
  114.4 15.8 %collective-permute-start.16 = (bf16[128,384]{1,0:T(8,128)(2,1)S(1)}, bf16[128,384]{1,0:T(8,128)(2,1)S(1)}, u32[]{:S(2)}, u32[]{:S(2)}) collective-permute-start(bf16[128,384]{1,0:T(8,128)(2,1)S(1)} %bitcast.40), channel_id=1, source_target_pairs={{2,0},{3,1},{0,2},{1,3},{6,4},{7,5},{4,6},{5,7},{10,8},{11,9},{8,1... | collective-permute-start | bytes 294920 | tf_op jit(solution)/shard_map/ppermute | solution.py:42
  126.2 5.2 %collective-permute-start.21 = (bf16[128,384]{1,0:T(8,128)(2,1)S(1)}, bf16[128,384]{1,0:T(8,128)(2,1)S(1)}, u32[]{:S(2)}, u32[]{:S(2)}) collective-permute-start(bf16[128,384]{1,0:T(8,128)(2,1)S(1)} %bitcast.34), channel_id=1, source_target_pairs={{12,0},{13,1},{14,2},{15,3},{0,4},{1,5},{2,6},{3,7},{4,8},{5,9},{6... | collective-permute-start | bytes 294920 | tf_op jit(solution)/shard_map/ppermute | solution.py:42
  128.6 25.1 %collective-permute-start.3 = (bf16[768,384]{1,0:T(8,128)(2,1)S(1)}, bf16[768,384]{1,0:T(8,128)(2,1)S(1)}, u32[]{:S(2)}, u32[]{:S(2)}) collective-permute-start(bf16[768,384]{1,0:T(8,128)(2,1)S(1)} %pad_maximum_fusion.1.refs_0_), channel_id=1, source_target_pairs={{12,0},{13,1},{14,2},{15,3},{0,4},{1,5},{2,6},{3,7},{4,8},{5,9},{6... | collective-permute-start | bytes 1769480 | tf_op jit(solution)/shard_map/ppermute | solution.py:42
  130.1 3.8 %collective-permute-start.22 = (bf16[128,384]{1,0:T(8,128)(2,1)S(1)}, bf16[128,384]{1,0:T(8,128)(2,1)S(1)}, u32[]{:S(2)}, u32[]{:S(2)}) collective-permute-start(bf16[128,384]{1,0:T(8,128)(2,1)S(1)} %bitcast.35), channel_id=1, source_target_pairs={{4,0},{5,1},{6,2},{7,3},{8,4},{9,5},{10,6},{11,7},{12,8},{13,9},{1... | collective-permute-start | bytes 294920 | tf_op jit(solution)/shard_map/ppermute | solution.py:42
  131.4 13.7 %collective-permute-start.23 = (bf16[128,384]{1,0:T(8,128)(2,1)S(1)}, bf16[128,384]{1,0:T(8,128)(2,1)S(1)}, u32[]{:S(2)}, u32[]{:S(2)}) collective-permute-start(bf16[128,384]{1,0:T(8,128)(2,1)S(1)} %bitcast.36), channel_id=1, source_target_pairs={{8,0},{9,1},{10,2},{11,3},{12,4},{13,5},{14,6},{15,7},{0,8},{1,9},... | collective-permute-start | bytes 294920 | tf_op jit(solution)/shard_map/ppermute | solution.py:42
  133.9 26.0 %collective-permute-start.4 = (bf16[768,384]{1,0:T(8,128)(2,1)S(1)}, bf16[768,384]{1,0:T(8,128)(2,1)}, u32[]{:S(2)}, u32[]{:S(2)}) collective-permute-start(bf16[768,384]{1,0:T(8,128)(2,1)S(1)} %pad_maximum_fusion.1.refs_0_), channel_id=1, source_target_pairs={{4,0},{5,1},{6,2},{7,3},{8,4},{9,5},{10,6},{11,7},{12,8},{13,9},{1... | collective-permute-start | bytes 1769480 | tf_op jit(solution)/shard_map/ppermute | solution.py:42
  145.1 17.2 %collective-permute-start.17 = (bf16[512,384]{1,0:T(8,128)(2,1)}, bf16[512,384]{1,0:T(8,128)(2,1)}, u32[]{:S(2)}, u32[]{:S(2)}) collective-permute-start(bf16[512,384]{1,0:T(8,128)(2,1)} %pad_maximum_fusion.3.refs_0_), channel_id=1, source_target_pairs={{12,0},{13,1},{14,2},{15,3},{0,4},{1,5},{2,6},{3,7},{4,8},{5,9},{6... | collective-permute-start | bytes 1179656 | tf_op jit(solution)/shard_map/ppermute | solution.py:42
  145.9 11.4 %copy-start.4 = (bf16[768,384]{1,0:T(8,128)(2,1)}, bf16[768,384]{1,0:T(8,128)(2,1)S(1)}, u32[]{:S(2)}) copy-start(bf16[768,384]{1,0:T(8,128)(2,1)S(1)} %collective-permute-done.10.refs_6_) | copy-start | bytes 1769476
  145.9 18.4 %collective-permute-start.18 = (bf16[512,384]{1,0:T(8,128)(2,1)}, bf16[512,384]{1,0:T(8,128)(2,1)}, u32[]{:S(2)}, u32[]{:S(2)}) collective-permute-start(bf16[512,384]{1,0:T(8,128)(2,1)} %pad_maximum_fusion.3.refs_0_), channel_id=1, source_target_pairs={{4,0},{5,1},{6,2},{7,3},{8,4},{9,5},{10,6},{11,7},{12,8},{13,9},{1... | collective-permute-start | bytes 1179656 | tf_op jit(solution)/shard_map/ppermute | solution.py:42
  148.6 16.1 %collective-permute-start.24 = (bf16[512,384]{1,0:T(8,128)(2,1)}, bf16[512,384]{1,0:T(8,128)(2,1)}, u32[]{:S(2)}, u32[]{:S(2)}) collective-permute-start(bf16[512,384]{1,0:T(8,128)(2,1)} %pad_maximum_fusion.4.refs_5_), channel_id=1, source_target_pairs={{3,0},{0,1},{1,2},{2,3},{7,4},{4,5},{5,6},{6,7},{11,8},{8,9},{9,10... | collective-permute-start | bytes 1179656 | tf_op jit(solution)/shard_map/ppermute | solution.py:42
  153.7 17.5 %collective-permute-start.25 = (bf16[512,384]{1,0:T(8,128)(2,1)}, bf16[512,384]{1,0:T(8,128)(2,1)}, u32[]{:S(2)}, u32[]{:S(2)}) collective-permute-start(bf16[512,384]{1,0:T(8,128)(2,1)} %pad_maximum_fusion.4.refs_5_), channel_id=1, source_target_pairs={{1,0},{2,1},{3,2},{0,3},{5,4},{6,5},{7,6},{4,7},{9,8},{10,9},{11,1... | collective-permute-start | bytes 1179656 | tf_op jit(solution)/shard_map/ppermute | solution.py:42
  158.0 38.3 %slice-start = ((s8[6291456]{0:T(1024)(128)(4,1)}), s8[2097152]{0:T(1024)(128)(4,1)S(1)}, s32[]{:S(2)}) async-start(s8[6291456]{0:T(1024)(128)(4,1)} %bitcast.24), calls=%async_computation.5 | async-start | bytes 4194304
  159.9 12.4 %collective-permute-start.12 = (bf16[384,384]{1,0:T(8,128)(2,1)}, bf16[384,384]{1,0:T(8,128)(2,1)}, u32[]{:S(2)}, u32[]{:S(2)}) collective-permute-start(bf16[384,384]{1,0:T(8,128)(2,1)} %slice.92), channel_id=1, source_target_pairs={{3,0},{0,1},{1,2},{2,3},{7,4},{4,5},{5,6},{6,7},{11,8},{8,9},{9,10... | collective-permute-start | bytes 884744 | tf_op jit(solution)/shard_map/ppermute | solution.py:42
  162.3 12.7 %collective-permute-start.13 = (bf16[384,384]{1,0:T(8,128)(2,1)}, bf16[384,384]{1,0:T(8,128)(2,1)}, u32[]{:S(2)}, u32[]{:S(2)}) collective-permute-start(bf16[384,384]{1,0:T(8,128)(2,1)} %slice.93), channel_id=1, source_target_pairs={{1,0},{2,1},{3,2},{0,3},{5,4},{6,5},{7,6},{4,7},{9,8},{10,9},{11,1... | collective-permute-start | bytes 884744 | tf_op jit(solution)/shard_map/ppermute | solution.py:42
  164.3 10.8 %collective-permute-start.5 = (bf16[384,384]{1,0:T(8,128)(2,1)}, bf16[384,384]{1,0:T(8,128)(2,1)}, u32[]{:S(2)}, u32[]{:S(2)}) collective-permute-start(bf16[384,384]{1,0:T(8,128)(2,1)} %slice.89), channel_id=1, source_target_pairs={{12,0},{13,1},{14,2},{15,3},{0,4},{1,5},{2,6},{3,7},{4,8},{5,9},{6... | collective-permute-start | bytes 884744 | tf_op jit(solution)/shard_map/ppermute | solution.py:42
  164.7 13.0 %collective-permute-start.6 = (bf16[384,384]{1,0:T(8,128)(2,1)}, bf16[384,384]{1,0:T(8,128)(2,1)}, u32[]{:S(2)}, u32[]{:S(2)}) collective-permute-start(bf16[384,384]{1,0:T(8,128)(2,1)} %slice.90), channel_id=1, source_target_pairs={{4,0},{5,1},{6,2},{7,3},{8,4},{9,5},{10,6},{11,7},{12,8},{13,9},{1... | collective-permute-start | bytes 884744 | tf_op jit(solution)/shard_map/ppermute | solution.py:42
  171.2 25.0 %collective-permute-start.19 = (bf16[256,384]{1,0:T(8,128)(2,1)S(1)}, bf16[256,384]{1,0:T(8,128)(2,1)S(1)}, u32[]{:S(2)}, u32[]{:S(2)}) collective-permute-start(bf16[256,384]{1,0:T(8,128)(2,1)S(1)} %slice.99), channel_id=1, source_target_pairs={{12,0},{13,1},{14,2},{15,3},{0,4},{1,5},{2,6},{3,7},{4,8},{5,9},{6... | collective-permute-start | bytes 589832 | tf_op jit(solution)/shard_map/ppermute | solution.py:42
  172.3 24.0 %collective-permute-start.20 = (bf16[256,384]{1,0:T(8,128)(2,1)S(1)}, bf16[256,384]{1,0:T(8,128)(2,1)S(1)}, u32[]{:S(2)}, u32[]{:S(2)}) collective-permute-start(bf16[256,384]{1,0:T(8,128)(2,1)S(1)} %slice.100), channel_id=1, source_target_pairs={{4,0},{5,1},{6,2},{7,3},{8,4},{9,5},{10,6},{11,7},{12,8},{13,9},{1... | collective-permute-start | bytes 589832 | tf_op jit(solution)/shard_map/ppermute | solution.py:42
  175.0 21.3 %collective-permute-start.26 = (bf16[256,384]{1,0:T(8,128)(2,1)S(1)}, bf16[256,384]{1,0:T(8,128)(2,1)S(1)}, u32[]{:S(2)}, u32[]{:S(2)}) collective-permute-start(bf16[256,384]{1,0:T(8,128)(2,1)S(1)} %slice.102), channel_id=1, source_target_pairs={{3,0},{0,1},{1,2},{2,3},{7,4},{4,5},{5,6},{6,7},{11,8},{8,9},{9,10... | collective-permute-start | bytes 589832 | tf_op jit(solution)/shard_map/ppermute | solution.py:42
  175.0 21.3 %collective-permute-start.27 = (bf16[256,384]{1,0:T(8,128)(2,1)S(1)}, bf16[256,384]{1,0:T(8,128)(2,1)S(1)}, u32[]{:S(2)}, u32[]{:S(2)}) collective-permute-start(bf16[256,384]{1,0:T(8,128)(2,1)S(1)} %slice.103), channel_id=1, source_target_pairs={{1,0},{2,1},{3,2},{0,3},{5,4},{6,5},{7,6},{4,7},{9,8},{10,9},{11,1... | collective-permute-start | bytes 589832 | tf_op jit(solution)/shard_map/ppermute | solution.py:42
  185.5 10.8 %copy-start.13 = (f32[256,128]{1,0:T(8,128)S(1)}, f32[256,128]{1,0:T(8,128)}, u32[]{:S(2)}) copy-start(f32[256,128]{1,0:T(8,128)} %fusion.12.refs_12_) | copy-start | bytes 393220
  185.5 10.8 %copy-start.14 = (f32[256,128]{1,0:T(8,128)S(1)}, f32[256,128]{1,0:T(8,128)}, u32[]{:S(2)}) copy-start(f32[256,128]{1,0:T(8,128)} %fusion.11.refs_13_) | copy-start | bytes 393220
  196.1 18.3 %slice-start.2 = ((s8[4718592]{0:T(1024)(128)(4,1)}), s8[4194304]{0:T(1024)(128)(4,1)S(1)}, s32[]{:S(2)}) async-start(s8[4718592]{0:T(1024)(128)(4,1)} %bitcast.27), calls=%async_computation.7 | async-start | bytes 8388608
  196.2 13.2 %copy-start.17 = (f32[640,128]{1,0:T(8,128)S(1)}, f32[640,128]{1,0:T(8,128)}, u32[]{:S(2)}) copy-start(f32[640,128]{1,0:T(8,128)} %pad_maximum_fusion.6.sin_ref) | copy-start | bytes 983044
  196.2 18.3 %slice-start.3 = ((s8[4718592]{0:T(1024)(128)(4,1)}), s8[524288]{0:T(1024)(128)(4,1)S(1)}, s32[]{:S(2)}) async-start(s8[4718592]{0:T(1024)(128)(4,1)} %bitcast.27), calls=%async_computation.8 | async-start | bytes 1048576
  196.2 11.2 %collective-permute-start.28 = (bf16[384,128]{1,0:T(8,128)(2,1)S(1)}, bf16[384,128]{1,0:T(8,128)(2,1)S(1)}, u32[]{:S(2)}, u32[]{:S(2)}) collective-permute-start(bf16[384,128]{1,0:T(8,128)(2,1)S(1)} %get-tuple-element.9.ot), channel_id=1, source_target_pairs={{0,1},{1,0},{2,3},{3,2},{4,5},{5,4},{6,7},{7,6},{8,9},{9,8},{10,11... | collective-permute-start | bytes 294920 | tf_op jit(solution)/shard_map/ppermute | solution.py:397
  206.0 3.4 collective-permute-start.29
  230.1 109.7 %copy-start.12 = (bf16[2,480,384]{2,1,0:T(8,128)(2,1)S(1)}, bf16[2,480,384]{2,1,0:T(8,128)(2,1)}, u32[]{:S(2)}) copy-start(bf16[2,480,384]{2,1,0:T(8,128)(2,1)} %text_ref.1) | copy-start | bytes 2211844
  230.1 10.0 %all-to-all-start.1 = ((bf16[16,2,384]{2,1,0:T(2,128)(2,1)}), bf16[16,2,384]{2,1,0:T(2,128)(2,1)S(1)}, u32[]{:S(2)}, u32[]{:S(2)}) async-start(bf16[16,2,384]{2,1,0:T(2,128)(2,1)} %bitcast.11), calls=%async_computation.2 | async-start | bytes 49152 | tf_op jit(solution)/shard_map/all_to_all | solution.py:427
  (19 other events, 84.7 us)
Sparse Core Ops, SparseCore 0:
  11.4 70.2 all-gather.4
  225.6 87.8 reduce-scatter.1
